TPU v7x, 32 devices: a whole 2x2x4 slice. The times are simulated.
32 devices in a mesh: gx: 2 (over y), gy: 4 (over x, core), col: 4 (over z).
Axes of the slice: x: 2, y: 2, z: 4, core: 2. Of those that a mesh axis runs over, the one named last changes fastest.
Arguments:
- vol_pts: float32 [3, 65536], P(None, ('gx', 'gy')), may hold values from 0 to 1
- surf_pts: float32 [3, 65536], P(None, 'col'), may hold values from 0 to 1
- surf_coef: float32 [3, 65536], P(None, 'col'), may hold values from -4 to 4
- vol_tile: int32 [32, 1024], P(('gx', 'gy', 'col')), may hold values from 0 to 63, as said below
- slot: int32 [32, 1024], P(('gx', 'gy', 'col')), may hold values from 0 to 127
- wanted: int32 [32, 4, 32], P(('gx', 'gy', 'col')), may hold values from 0 to 127, as said below
- live: int32 [32], P(('gx', 'gy', 'col')), may hold values from 256 to 1024, as said below
Outputs:
- displacement: float32 [3, 65536], P(None, ('gx', 'gy', 'col'))
Inputs may be any that keep to these rules, and one draw needn't show every extreme that they name: Within one device the pairs (vol_tile, slot) are distinct. `wanted`: the 32 tiles one device requests from one index of col are distinct. Only the first live[d] slots of device d are pairs; some device has all 1024 live.
All inputs are finite; a program needn't handle non-finite values.
Results may differ from a plain program's by a relative error of at most 0.0003.
Values sent between devices are 32-bit elements; how exact they have to be, the bound alone decides.
No kernel may reach another device: no remote copies, remote signals or barrier semaphores. Data moves between devices by JAX's collectives and lax.ppermute only.
A program may use at most 64 MiB of HBM per device.

v0:
```python
import jax
import jax.numpy as jnp
from jax import lax
from jax.sharding import PartitionSpec as P

TILE = 128
PB = 16


def per_device(vol_pts, surf_pts, surf_coef, vol_tile, slot, wanted, live):
    col_count = lax.axis_size("col")
    vol_tiles = vol_pts.reshape(3, -1, TILE).transpose(1, 0, 2)
    group_tiles = vol_tiles.shape[0]
    local_tiles = jnp.concatenate([surf_pts, surf_coef], 0).reshape(6, -1, TILE).transpose(1, 0, 2)
    requested = wanted[0]
    gathered = lax.all_gather(local_tiles, "col", axis=0, tiled=True)
    peers = jnp.arange(col_count, dtype=jnp.int32)[:, None] * local_tiles.shape[0]
    slot_tile = (peers + requested).reshape(-1)
    source = gathered[slot_tile]
    pair_vol = vol_tile[0]
    pair_slot = slot[0]
    live_count = live[0]
    blocks = (live_count + PB - 1) // PB
    tile_ids = jnp.arange(group_tiles, dtype=jnp.int32)

    def add_block(block, totals):
        offset = block * PB
        vol_index = lax.dynamic_slice_in_dim(pair_vol, offset, PB)
        src_index = lax.dynamic_slice_in_dim(pair_slot, offset, PB)
        points = vol_tiles[vol_index]
        sources = source[src_index]
        squared = jnp.zeros((PB, TILE, TILE), jnp.float32)
        for comp in range(3):
            diff = points[:, comp, :, None] - sources[:, comp, None, :]
            squared = squared + diff * diff
        radius = jnp.sqrt(squared) / 1.2
        falloff = jnp.maximum(1.0 - radius, 0.0)
        kernel = falloff**4 * (4.0 * radius + 1.0)
        is_live = offset + jnp.arange(PB, dtype=jnp.int32) < live_count
        kernel = jnp.where(is_live[:, None, None], kernel, 0.0)
        motion = jnp.einsum("pij,pkj->pki", kernel, sources[:, 3:], precision=lax.Precision.HIGHEST)
        one_hot = (vol_index[:, None] == tile_ids[None, :]).astype(jnp.float32)
        return totals + jnp.dot(one_hot.T, motion.reshape(PB, -1), precision=lax.Precision.HIGHEST)

    empty = jnp.zeros((group_tiles, 3 * TILE), jnp.float32)
    totals = lax.fori_loop(0, blocks, add_block, empty)
    whole = lax.psum(totals, "col")
    share = group_tiles // col_count
    mine = lax.dynamic_slice_in_dim(whole, lax.axis_index("col") * share, share, 0)
    return mine.reshape(-1, 3, TILE).transpose(1, 0, 2).reshape(3, -1)


def solution(mesh):
    return jax.shard_map(
        per_device,
        mesh=mesh,
        in_specs=(
            P(None, ("gx", "gy")),
            P(None, "col"),
            P(None, "col"),
            P(("gx", "gy", "col"), None),
            P(("gx", "gy", "col"), None),
            P(("gx", "gy", "col"), None, None),
            P(("gx", "gy", "col")),
        ),
        out_specs=P(None, ("gx", "gy", "col")),
        check_vma=False,
    )
```

profile of v0, /device:TPU:0, one launch (start us, length us, event | category | flops | bytes accessed | tf_op | source)
XLA Modules:
  0.0 518.0 jit_solution(8472771384200588862)
XLA Ops:
  9.5 39.2 %all-gather.2.cloned.1.call-done = f32[512,6,128]{2,0,1:T(8,128)} async-done(((f32[128,6,128]{2,0,1:T(8,128)}), f32[512,6,128]{2,0,1:T(8,128)}) %all-gather.2.cloned.1.call-update) | async-done | bytes 1572880 | tf_op jit(solution)/shard_map/all_gather | solution.py:16
  51.9 311.9 %while.13 = (s32[]{:T(128)}, f32[64,384]{1,0:T(8,128)S(1)}, s32[]{:T(128)}, s32[1024]{0:T(1024)}, s32[1024]{0:T(1024)}, /*index=5*/f32[128,6,128]{2,1,0:T(8,128)...) while((s32[]{:T(128)}, f32[64,384]{1,0:T(8,128)S(1)}, ...), condition=%wide.region_1.2_spmd.clone, body=%wide.region_0.1_spmd.clone.sunk | while | flops 18640004 | bytes 582975 | solution.py:46
  55.5 2.7 fusion.54
  68.8 2.7 fusion.54
  75.4 2.7 fusion.54
  82.0 2.7 fusion.54
  88.7 2.7 fusion.54
  95.3 2.7 fusion.54
  102.0 2.7 fusion.54
  108.6 2.7 fusion.54
  115.2 2.7 fusion.54
  121.9 2.7 fusion.54
  128.5 2.7 fusion.54
  135.1 2.7 fusion.54
  141.8 2.7 fusion.54
  148.4 2.7 fusion.54
  155.0 2.7 fusion.54
  161.7 2.7 fusion.54
  168.3 2.7 fusion.54
  181.6 2.7 fusion.54
  188.2 2.7 fusion.54
  194.9 2.7 fusion.54
  201.5 2.7 fusion.54
  364.5 145.3 %all-reduce.2.cloned.1.call-done = f32[64,384]{1,0:T(8,128)} async-done(((f32[64,384]{1,0:T(8,128)}), f32[64,384]{1,0:T(8,128)}) %all-reduce.2.cloned.1.call-update) | async-done | bytes 98320 | tf_op jit(solution)/shard_map/psum | solution.py:47
  (470 shorter events, 259.9 us)
Async XLA Ops:
  6.5 2.9 copy-start.1
  6.5 42.2 %all-gather.2.cloned.1.call-start = ((), (), s32[]{:S(2)}) async-start(), calls=%async_computation | async-start | bytes 1966080 | tf_op jit(solution)/shard_map/all_gather | solution.py:16
  8.5 501.2 %all-reduce.2.cloned.1.call-start = ((), (), s32[]{:S(2)}) async-start(), calls=%async_computation.1 | async-start | bytes 196608 | tf_op jit(solution)/shard_map/psum | solution.py:47
  363.8 0.6 copy-start
Sparse Core Ops, SparseCore 0:
  8.9 39.7 all-gather.1
  364.6 145.1 all-reduce.1
where the time goes:
time: 523 us; the launch traced here: 518 us
  waiting for transfers between devices  185 us (35%)
  matrix products  142 us (27%)
  local copies, waits for them, and re-layouts  105 us (20%)
  other arithmetic  69.3 us (13%)
  between operations  14.1 us (3%)
    psum x1, waiting for transfers between devices, per_device(): whole = lax.psum(totals, 'col')  145 us
    dot_general x47, matrix products, add_block(): jnp.einsum('pij,pkj->pki', kernel, sources[:, 3:], precision=lax.Precisio...  126 us
    gather x47, local copies, waits for them, and re-layouts, add_block(): points = vol_tiles[vol_index]  70.2 us
    all_gather x1, waiting for transfers between devices, per_device(): gathered = lax.all_gather(local_tiles, 'col', axis=0, tiled=True)  39.2 us
    select_n x47, other arithmetic, add_block(): points = vol_tiles[vol_index]  36.8 us
    lt x47, other arithmetic, add_block(): is_live = offset + jnp.arange(PB, dtype=jnp.int32) < live_count  30.7 us
    gather x47, local copies, waits for them, and re-layouts, add_block(): sources = source[src_index]  26.6 us
    dot_general x47, matrix products, add_block(): jnp.dot(one_hot.T, motion.reshape(PB, -1), precision=lax.Precision.HIGHEST)  16.3 us
  transfers between devices with their start and end apart: 2, of which 2 were waited for; matrix products, arithmetic and copies ran while one was open for 0% of the time, Pallas kernels for 0%

commit v1 on v0

v1 whole, which is shorter than its diff:
```python
import functools

import jax
import jax.numpy as jnp
from jax import lax
from jax.experimental import pallas as pl
from jax.experimental.pallas import tpu as pltpu
from jax.sharding import PartitionSpec as P

TILE = 128
RADIUS = 1.2
FEATS = 32
UNROLL = 8
F32, BF16, I32 = jnp.float32, jnp.bfloat16, jnp.int32


def dot(a, b, contract=((1,), (0,))):
    return lax.dot_general(a, b, (contract, ((), ())), preferred_element_type=F32)


def iota(shape, axis):
    return lax.broadcasted_iota(I32, shape, axis)


def sort_kernel(n_col, n_local, live_ref, vol_ref, slot_ref, wanted_ref, msg_ref):
    rows = vol_ref.shape[0]
    slots = wanted_ref.shape[1]
    req = slots // n_col
    slot = slot_ref[...]
    vol = vol_ref[...].astype(F32)
    position = iota((rows, TILE), 0) * TILE + iota((rows, TILE), 1)
    key = jnp.where(position < live_ref[0], slot // req, n_col)
    keys = n_col + 1
    keys += keys % 2
    masks = [(key == k).astype(F32) for k in range(keys)]
    mask = jnp.concatenate(masks, 0).astype(BF16)
    ahead = (iota((TILE, TILE), 0) < iota((TILE, TILE), 1)).astype(F32).astype(BF16)
    within = dot(mask, ahead)
    count = dot(mask, jnp.ones((TILE, TILE), BF16)).astype(BF16)
    total = keys * rows
    above = (iota((total, total), 1) < iota((total, total), 0)).astype(F32).astype(BF16)
    start = dot(above, count)
    rank = within + start
    dest = masks[0] * rank[:rows]
    for k in range(1, keys):
        dest += masks[k] * rank[k * rows : (k + 1) * rows]
    dest = dest.astype(I32)
    dest_row, dest_lane = dest // TILE, dest % TILE
    table = jnp.broadcast_to(wanted_ref[...], (8, slots)).astype(F32).astype(BF16)
    out = jnp.zeros((2 * rows, TILE), F32)
    for r in range(rows):
        row = slice(r, r + 1)
        chosen = (iota((slots, TILE), 0) == slot[row]).astype(F32).astype(BF16)
        tile = dot(table, chosen)[:1]
        here = (iota((rows, TILE), 0) == dest_row[row]).astype(F32)
        values = jnp.concatenate([here * vol[row], here * tile], 0).astype(BF16)
        lanes = (iota((TILE, TILE), 0) == dest_lane[row]).astype(F32).astype(BF16)
        out += dot(values, lanes, ((1,), (1,)))
    out = out.astype(I32)
    msg_ref[:rows] = out[:rows] * n_local + out[rows:]
    tail = jnp.concatenate([start[k * rows : k * rows + 1] for k in range(keys)], 0)
    pad = msg_ref.shape[0] - rows - keys
    if pad:
        tail = jnp.concatenate([tail, jnp.zeros((pad, TILE), F32)], 0)
    msg_ref[rows:] = tail.astype(I32)


def thirds(a):
    one = a.astype(BF16).astype(F32)
    two = (a - one).astype(BF16).astype(F32)
    return one, two, a - one - two


def point_features(points):
    a = (points - 0.5) * (1.0 / RADIUS)
    norm = a[0:1] * a[0:1] + a[1:2] * a[1:2] + a[2:3] * a[2:3]
    return thirds(a), jnp.concatenate(thirds(norm), 0)


def main_kernel(
    n_col, n_local, list_rows, me_ref, *refs
):
    msgs = refs[:n_col]
    vol_ref, pts_ref, coef_ref = refs[n_col : n_col + 3]
    outs = refs[n_col + 3 : 2 * n_col + 3]
    lists, flat, surf, vols, coefs, acc, dist, kern, sems = refs[2 * n_col + 3 :]
    msg_rows = msgs[0].shape[0]
    copies = [
        pltpu.make_async_copy(msgs[k], lists.at[pl.ds(k * msg_rows, msg_rows)], sems.at[k])
        for k in range(n_col)
    ]
    for c in copies:
        c.start()
    acc[...] = jnp.zeros_like(acc)

    group_tiles = vols.shape[0]
    step = 8
    ones = jnp.ones((3, step * TILE), F32)
    blank = jnp.zeros((FEATS - 24, step * TILE), F32)

    def surface(b, _):
        lanes = pl.ds(pl.multiple_of(b * step * TILE, step * TILE), step * TILE)
        (one, two, three), norm = point_features(pts_ref[:, lanes])
        one, two, three = -2.0 * one, -2.0 * two, -2.0 * three
        rows = jnp.concatenate([one, two, one, three, one, two, norm, ones, blank], 0)
        coef = coef_ref[:, lanes] * 4.0
        high = coef.astype(BF16).astype(F32)
        pair = jnp.concatenate([high, coef - high, jnp.zeros((2, step * TILE), F32)], 0)
        for t in range(step):
            span = slice(t * TILE, (t + 1) * TILE)
            surf[b * step + t] = rows[:, span].T.astype(BF16)
            tile = pair[:, span].astype(BF16)
            coefs[b * step + t] = jnp.concatenate([tile, tile], 1)
        return 0

    lax.fori_loop(0, n_local // step, surface, 0)
    surf[n_local] = jnp.zeros((TILE, FEATS), BF16)
    coefs[n_local] = jnp.zeros((8, 2 * TILE), BF16)

    def volume(b, _):
        lanes = pl.ds(pl.multiple_of(b * step * TILE, step * TILE), step * TILE)
        (one, two, three), norm = point_features(vol_ref[:, lanes])
        rows = jnp.concatenate([one, one, two, one, three, two, ones, norm, blank], 0).astype(BF16)
        for t in range(step):
            vols[b * step + t] = rows[:, t * TILE : (t + 1) * TILE]
        return 0

    lax.fori_loop(0, group_tiles // step, volume, 0)

    for c in copies:
        c.wait()
    me = me_ref[0]
    ends, shifts = [], []
    total = jnp.int32(0)
    for k in range(n_col):
        first = lists[k * msg_rows + list_rows + me, 0]
        last = lists[k * msg_rows + list_rows + me + 1, 0]
        shifts.append(k * msg_rows * TILE + first - total)
        total = total + (last - first)
        ends.append(total)

    def fetch(p):
        shift = shifts[0]
        for k in range(1, n_col):
            shift = jnp.where(p >= ends[k - 1], shifts[k], shift)
        valid = p < total
        at = jnp.where(valid, p + shift, 0)
        pair = lists[at // TILE, at % TILE]
        pair = jnp.where(valid, pair, -1)
        flat[p] = pair
        return pair

    def parts(pair):
        valid = pair >= 0
        return (
            jnp.where(valid, pair // n_local, 0),
            jnp.where(valid, pair % n_local, n_local),
        )

    def distances(b, slot):
        for q in range(UNROLL):
            v, s = parts(fetch(b * UNROLL + q))
            dist[slot, q] = dot(surf[s], vols[v])

    def kernels(slot):
        for q in range(UNROLL):
            squared = jnp.minimum(jnp.maximum(dist[slot, q], 1e-12), 1.0)
            radius = squared * lax.rsqrt(squared)
            falloff = 1.0 - radius
            falloff = falloff * falloff
            value = falloff * falloff * (radius + 0.25)
            high = value.astype(BF16)
            kern[slot, q, :TILE] = high
            kern[slot, q, TILE:] = (value - high.astype(F32)).astype(BF16)

    def motions(b, slot):
        for q in range(UNROLL):
            v, s = parts(flat[b * UNROLL + q])
            acc[v] += dot(coefs[s], kern[slot, q])

    trips = jnp.maximum((total + 2 * UNROLL - 1) // (2 * UNROLL), 1)
    distances(0, 0)
    kernels(0)
    distances(1, 1)

    def trip(h, _):
        b = 2 * h
        motions(b - 2, 0)
        kernels(1)
        distances(b, 0)
        motions(b - 1, 1)
        kernels(0)
        distances(b + 1, 1)
        return 0

    lax.fori_loop(1, trips, trip, 0)
    b = 2 * trips
    motions(b - 2, 0)
    kernels(1)
    motions(b - 1, 1)

    share = group_tiles // n_col
    for k in range(n_col):
        base = lax.rem(me + k, n_col) * share
        for t in range(share):
            value = acc[base + t]
            outs[k][:, t * TILE : (t + 1) * TILE] = value[:3] + value[3:6]


def shift_right(x, k, n):
    return lax.ppermute(x, "col", [(i, (i + k) % n) for i in range(n)])


def per_device(vol_pts, surf_pts, surf_coef, vol_tile, slot, wanted, live):
    n_col = lax.axis_size("col")
    me = lax.axis_index("col").astype(I32).reshape(1)
    n_local = surf_pts.shape[1] // TILE
    group_tiles = vol_pts.shape[1] // TILE
    share = group_tiles // n_col
    list_rows = vol_tile.shape[1] // TILE
    msg_rows = -(-(list_rows + n_col + 2) // 8) * 8
    smem = pl.BlockSpec(memory_space=pltpu.SMEM)
    vmem = pl.BlockSpec(memory_space=pltpu.VMEM)
    msg = pl.pallas_call(
        functools.partial(sort_kernel, n_col, n_local),
        out_shape=jax.ShapeDtypeStruct((msg_rows, TILE), I32),
        in_specs=[smem, vmem, vmem, vmem],
        out_specs=vmem,
        name="sort_pairs",
    )(live, vol_tile.reshape(-1, TILE), slot.reshape(-1, TILE), wanted.reshape(1, -1))
    msgs = [msg] + [shift_right(msg, k, n_col) for k in range(1, n_col)]
    room = n_col * list_rows * TILE + 4 * UNROLL
    parts = pl.pallas_call(
        functools.partial(main_kernel, n_col, n_local, list_rows),
        out_shape=[jax.ShapeDtypeStruct((3, share * TILE), F32)] * n_col,
        in_specs=[smem] + [pl.BlockSpec(memory_space=pl.ANY)] * n_col + [vmem] * 3,
        out_specs=[vmem] * n_col,
        scratch_shapes=[
            pltpu.SMEM((n_col * msg_rows, TILE), I32),
            pltpu.SMEM((room,), I32),
            pltpu.VMEM((n_local + 1, TILE, FEATS), BF16),
            pltpu.VMEM((group_tiles, FEATS, TILE), BF16),
            pltpu.VMEM((n_local + 1, 8, 2 * TILE), BF16),
            pltpu.VMEM((group_tiles, 8, TILE), F32),
            pltpu.VMEM((2, UNROLL, TILE, TILE), F32),
            pltpu.VMEM((2, UNROLL, 2 * TILE, TILE), BF16),
            pltpu.SemaphoreType.DMA((n_col,)),
        ],
        compiler_params=pltpu.CompilerParams(vmem_limit_bytes=48 << 20),
        name="pair_sums",
    )(me, *msgs, vol_pts, surf_pts, surf_coef)
    out = parts[0]
    for k in range(1, n_col):
        out = out + shift_right(parts[k], k, n_col)
    return out


def solution(mesh):
    return jax.shard_map(
        per_device,
        mesh=mesh,
        in_specs=(
            P(None, ("gx", "gy")),
            P(None, "col"),
            P(None, "col"),
            P(("gx", "gy", "col"), None),
            P(("gx", "gy", "col"), None),
            P(("gx", "gy", "col"), None, None),
            P(("gx", "gy", "col")),
        ),
        out_specs=P(None, ("gx", "gy", "col")),
        check_vma=False,
    )
```

time: 523 us -> 59.3 us (0.11)
  the two profiles are of different devices: /device:TPU:0 before, /device:TPU:14 now
where the time goes in v1:
time: 59.3 us; the launch traced here: 59.2 us
  Pallas kernels  37 us (62%)
  starting transfers between devices  10.7 us (18%)
  waiting for transfers between devices  5.34 us (9%)
  local copies, waits for them, and re-layouts  4.8 us (8%)
  between operations  0.67 us (1%)
  other arithmetic  0.64 us (1%)
    pallas_call x1, Pallas kernels, per_device(): pl.pallas_call(functools.partial(main_kernel, n_col, n_local, list_rows),...  34.9 us
    ppermute x6, starting transfers between devices, shift_right(): return lax.ppermute(x, 'col', [(i, (i + k) % n) for i in range(n)])  10.7 us
    ppermute x6, waiting for transfers between devices, shift_right(): return lax.ppermute(x, 'col', [(i, (i + k) % n) for i in range(n)])  5.34 us
    unnamed x8, local copies, waits for them, and re-layouts  3.5 us
    pallas_call x1, Pallas kernels, per_device(): pl.pallas_call(functools.partial(sort_kernel, n_col, n_local), out_shape=...  2.09 us
    reshape x1, local copies, waits for them, and re-layouts, per_device(): wanted.reshape(1, -1)  1.3 us
  transfers between devices with their start and end apart: 6, of which 3 were waited for; matrix products, arithmetic and copies ran while one was open for 0% of the time, Pallas kernels for 0%

profile of v1, /device:TPU:14, one launch (start us, length us, event | category | flops | bytes accessed | tf_op | source)
XLA Modules:
  0.0 59.2 jit_solution(13503076224381585485)
XLA Ops:
  0.7 1.3 %reshape.15.wanted_ref = s32[1,128]{1,0:T(1,128)} reshape(s32[1,4,32]{2,1,0:T(4,128)} %param.12) | data formatting | bytes 1024 | tf_op jit(solution)/shard_map/reshape | solution.py:230
  2.0 2.1 %sort_pairs.1.refs_0_ = s32[16,128]{1,0:T(8,128)} custom-call(s32[1]{0:T(128)S(6)} %copy.8.live_ref, s32[8,128]{1,0:T(8,128)} %bitcast.3, s32[8,128]{1,0:T(8,128)} %bitcast.4, s32[1,128]{1,0:T(1,128)} %reshape.15.wanted_ref), custom_call_target="tpu_custom_call" | custom-call | tf_op jit(solution)/shard_map/sort_pairs/pallas_call | solution.py:224
  4.0 0.4 collective-permute-start.2
  4.5 2.6 %collective-permute-start.1 = (s32[16,128]{1,0:T(8,128)}, s32[16,128]{1,0:T(8,128)S(1)}, u32[]{:S(2)}, u32[]{:S(2)}) collective-permute-start(s32[16,128]{1,0:T(8,128)} %sort_pairs.1.refs_0_), channel_id=1, source_target_pairs={{0,2},{1,3},{2,0},{3,1},{4,6},{5,7},{6,4},{7,5},{8,10},{9,11},{10,... | collective-permute-start | bytes 24584 | tf_op jit(solution)/shard_map/ppermute | solution.py:211
  7.1 2.5 %collective-permute-start = (s32[16,128]{1,0:T(8,128)}, s32[16,128]{1,0:T(8,128)S(1)}, u32[]{:S(2)}, u32[]{:S(2)}) collective-permute-start(s32[16,128]{1,0:T(8,128)} %sort_pairs.1.refs_0_), channel_id=1, source_target_pairs={{0,1},{1,2},{2,3},{3,0},{4,5},{5,6},{6,7},{7,4},{8,9},{9,10},{10,1... | collective-permute-start | bytes 24584 | tf_op jit(solution)/shard_map/ppermute | solution.py:211
  9.6 0.0 collective-permute-done.2.refs_3_
  9.6 0.0 collective-permute-done.1.refs_2_
  9.6 1.6 %collective-permute-done.refs_1_ = s32[16,128]{1,0:T(8,128)S(1)} collective-permute-done((s32[16,128]{1,0:T(8,128)}, s32[16,128]{1,0:T(8,128)S(1)}, u32[]{:S(2)}, u32[]{:S(2)}) %collective-permute-start) | collective-permute-done | bytes 8224 | tf_op jit(solution)/shard_map/ppermute | solution.py:211
  11.1 0.0 copy-start
  11.1 0.9 %copy-done = f32[3,16384]{1,0:T(4,128)S(1)} copy-done((f32[3,16384]{1,0:T(4,128)S(1)}, f32[3,16384]{1,0:T(4,128)}, u32[]{:S(2)}) %copy-start) | copy-done | bytes 196632
  12.1 0.0 copy-start.1
  12.1 0.9 %copy-done.1 = f32[3,16384]{1,0:T(4,128)S(1)} copy-done((f32[3,16384]{1,0:T(4,128)S(1)}, f32[3,16384]{1,0:T(4,128)}, u32[]{:S(2)}) %copy-start.1) | copy-done | bytes 196632
  13.0 0.0 copy-start.2
  13.0 0.9 %copy-done.2 = f32[3,8192]{1,0:T(4,128)S(1)} copy-done((f32[3,8192]{1,0:T(4,128)S(1)}, f32[3,8192]{1,0:T(4,128)}, u32[]{:S(2)}) %copy-start.2) | copy-done | bytes 98328
  13.9 0.0 copy-start.3
  13.9 0.7 %copy-done.3 = s32[16,128]{1,0:T(8,128)S(1)} copy-done((s32[16,128]{1,0:T(8,128)S(1)}, s32[16,128]{1,0:T(8,128)}, u32[]{:S(2)}) %copy-start.3) | copy-done | bytes 8216
  14.6 34.9 %pair_sums.1 = (f32[3,2048]{1,0:T(4,128)S(1)}, f32[3,2048]{1,0:T(4,128)S(1)}, f32[3,2048]{1,0:T(4,128)S(1)}, f32[3,2048]{1,0:T(4,128)S(1)}) custom-call(s32[1]{0:T(128)} %bitcast.me_ref, s32[16,128]{1,0:T(8,128)S(1)} %copy-done.3, s32[16,128]{1,0:T(8,128)S(1)} %collective-permute-done.refs_1_, s32[16,128]{1,0:T(8,128)S(1)} %collective-permute-done.1.refs_2_, ...), custom_call_target="tpu_custom_call" | custom-call | tf_op jit(solution)/shard_map/pair_sums/pallas_call | solution.py:233
  49.6 2.4 %collective-permute-start.3 = (f32[3,2048]{1,0:T(4,128)S(1)}, f32[3,2048]{1,0:T(4,128)S(1)}, u32[]{:S(2)}, u32[]{:S(2)}) collective-permute-start(f32[3,2048]{1,0:T(4,128)S(1)} %get-tuple-element.10), channel_id=1, source_target_pairs={{0,1},{1,2},{2,3},{3,0},{4,5},{5,6},{6,7},{7,4},{8,9},{9,10},{10,1... | collective-permute-start | bytes 73736 | tf_op jit(solution)/shard_map/ppermute | solution.py:211
  51.9 2.7 %collective-permute-start.4 = (f32[3,2048]{1,0:T(4,128)S(1)}, f32[3,2048]{1,0:T(4,128)S(1)}, u32[]{:S(2)}, u32[]{:S(2)}) collective-permute-start(f32[3,2048]{1,0:T(4,128)S(1)} %get-tuple-element.11), channel_id=1, source_target_pairs={{0,2},{1,3},{2,0},{3,1},{4,6},{5,7},{6,4},{7,5},{8,10},{9,11},{10,... | collective-permute-start | bytes 73736 | tf_op jit(solution)/shard_map/ppermute | solution.py:211
  54.6 0.1 collective-permute-start.5
  54.8 0.0 collective-permute-done.3
  54.8 2.1 %collective-permute-done.4 = f32[3,2048]{1,0:T(4,128)S(1)} collective-permute-done((f32[3,2048]{1,0:T(4,128)S(1)}, f32[3,2048]{1,0:T(4,128)S(1)}, u32[]{:S(2)}, u32[]{:S(2)}) %collective-permute-start.4) | collective-permute-done | bytes 24608 | tf_op jit(solution)/shard_map/ppermute | solution.py:211
  56.9 1.7 %collective-permute-done.5 = f32[3,2048]{1,0:T(4,128)S(1)} collective-permute-done((f32[3,2048]{1,0:T(4,128)S(1)}, f32[3,2048]{1,0:T(4,128)S(1)}, u32[]{:S(2)}, u32[]{:S(2)}) %collective-permute-start.5) | collective-permute-done | bytes 24608 | tf_op jit(solution)/shard_map/ppermute | solution.py:211
  58.5 0.6 %add_add_fusion = f32[3,2048]{1,0:T(4,128)} fusion(f32[3,2048]{1,0:T(4,128)S(1)} %collective-permute-done.5, f32[3,2048]{1,0:T(4,128)S(1)} %collective-permute-done.4, f32[3,2048]{1,0:T(4,128)S(1)} %get-tuple-element.9, f32[3,2048]{1,0:T(4,128)S(1)} %collective-permute-done.3), kind=kLoop, calls=%fused_computation | loop fusion | flops 18432 | bytes 122880 | tf_op jit(solution)/shard_map/add | solution.py:254
Async XLA Ops:
  4.0 5.5 %collective-permute-start.2 = (s32[16,128]{1,0:T(8,128)}, s32[16,128]{1,0:T(8,128)S(1)}, u32[]{:S(2)}, u32[]{:S(2)}) collective-permute-start(s32[16,128]{1,0:T(8,128)} %sort_pairs.1.refs_0_), channel_id=1, source_target_pairs={{0,3},{1,0},{2,1},{3,2},{4,7},{5,4},{6,5},{7,6},{8,11},{9,8},{10,9... | collective-permute-start | bytes 24584 | tf_op jit(solution)/shard_map/ppermute | solution.py:211
  4.5 5.1 %collective-permute-start.1 = (s32[16,128]{1,0:T(8,128)}, s32[16,128]{1,0:T(8,128)S(1)}, u32[]{:S(2)}, u32[]{:S(2)}) collective-permute-start(s32[16,128]{1,0:T(8,128)} %sort_pairs.1.refs_0_), channel_id=1, source_target_pairs={{0,2},{1,3},{2,0},{3,1},{4,6},{5,7},{6,4},{7,5},{8,10},{9,11},{10,... | collective-permute-start | bytes 24584 | tf_op jit(solution)/shard_map/ppermute | solution.py:211
  7.1 4.1 %collective-permute-start = (s32[16,128]{1,0:T(8,128)}, s32[16,128]{1,0:T(8,128)S(1)}, u32[]{:S(2)}, u32[]{:S(2)}) collective-permute-start(s32[16,128]{1,0:T(8,128)} %sort_pairs.1.refs_0_), channel_id=1, source_target_pairs={{0,1},{1,2},{2,3},{3,0},{4,5},{5,6},{6,7},{7,4},{8,9},{9,10},{10,1... | collective-permute-start | bytes 24584 | tf_op jit(solution)/shard_map/ppermute | solution.py:211
  11.1 0.9 %copy-start = (f32[3,16384]{1,0:T(4,128)S(1)}, f32[3,16384]{1,0:T(4,128)}, u32[]{:S(2)}) copy-start(f32[3,16384]{1,0:T(4,128)} %refs_5_.1) | copy-start | bytes 589828
  12.1 0.9 %copy-start.1 = (f32[3,16384]{1,0:T(4,128)S(1)}, f32[3,16384]{1,0:T(4,128)}, u32[]{:S(2)}) copy-start(f32[3,16384]{1,0:T(4,128)} %refs_6_.1) | copy-start | bytes 589828
  13.0 0.9 %copy-start.2 = (f32[3,8192]{1,0:T(4,128)S(1)}, f32[3,8192]{1,0:T(4,128)}, u32[]{:S(2)}) copy-start(f32[3,8192]{1,0:T(4,128)} %refs_4_.1) | copy-start | bytes 294916
  13.9 0.7 %copy-start.3 = (s32[16,128]{1,0:T(8,128)S(1)}, s32[16,128]{1,0:T(8,128)}, u32[]{:S(2)}) copy-start(s32[16,128]{1,0:T(8,128)} %sort_pairs.1.refs_0_) | copy-start | bytes 24580
  49.6 5.2 %collective-permute-start.3 = (f32[3,2048]{1,0:T(4,128)S(1)}, f32[3,2048]{1,0:T(4,128)S(1)}, u32[]{:S(2)}, u32[]{:S(2)}) collective-permute-start(f32[3,2048]{1,0:T(4,128)S(1)} %get-tuple-element.10), channel_id=1, source_target_pairs={{0,1},{1,2},{2,3},{3,0},{4,5},{5,6},{6,7},{7,4},{8,9},{9,10},{10,1... | collective-permute-start | bytes 73736 | tf_op jit(solution)/shard_map/ppermute | solution.py:211
  51.9 4.9 %collective-permute-start.4 = (f32[3,2048]{1,0:T(4,128)S(1)}, f32[3,2048]{1,0:T(4,128)S(1)}, u32[]{:S(2)}, u32[]{:S(2)}) collective-permute-start(f32[3,2048]{1,0:T(4,128)S(1)} %get-tuple-element.11), channel_id=1, source_target_pairs={{0,2},{1,3},{2,0},{3,1},{4,6},{5,7},{6,4},{7,5},{8,10},{9,11},{10,... | collective-permute-start | bytes 73736 | tf_op jit(solution)/shard_map/ppermute | solution.py:211
  54.6 3.9 %collective-permute-start.5 = (f32[3,2048]{1,0:T(4,128)S(1)}, f32[3,2048]{1,0:T(4,128)S(1)}, u32[]{:S(2)}, u32[]{:S(2)}) collective-permute-start(f32[3,2048]{1,0:T(4,128)S(1)} %get-tuple-element.12), channel_id=1, source_target_pairs={{0,3},{1,0},{2,1},{3,2},{4,7},{5,4},{6,5},{7,6},{8,11},{9,8},{10,9... | collective-permute-start | bytes 73736 | tf_op jit(solution)/shard_map/ppermute | solution.py:211
